TPU v7x, 256 devices: a whole 4x4x8 slice. The times are simulated.
256 devices in a mesh: seq: 32 (over y, z), mp: 8 (over x, core).
Axes of the slice: x: 4, y: 4, z: 8, core: 2. Of those that a mesh axis runs over, the one named last changes fastest.
Arguments:
- hidden: bfloat16 [4, 16384, 8192], P(None, 'seq', 'mp'), may hold values from -1000 to 1000
- norm_gain: bfloat16 [4, 8192], P(None, 'mp'), may hold values from 0.25 to 1.75
- proj_weight: bfloat16 [4, 8192, 1024], P(None, 'mp'), may hold values from -0.0625 to 0.0625
- start_block: bfloat16 [8, 512, 128], replicated, may hold values from -6 to 6
Outputs:
- latents: bfloat16 [16384, 8, 128], P('seq', 'mp')
All inputs are finite; a program needn't handle non-finite values.
Results may differ from a plain program's by a relative error of at most 0.025.
Values may be sent and summed in bfloat16 or wider, within the bound.
A program may use at most 64 MiB of HBM per device.

v0:
```python
import jax
import jax.numpy as jnp
from jax import lax
from jax.sharding import PartitionSpec as P

D = 8192
HD = 128
ITERS = 2


epsilon = 1e-05
highest_precision = lax.Precision.HIGHEST


def orthonormal_basis(image_block):
    inner_block = jnp.einsum("sar,saq->srq", image_block, image_block, precision=highest_precision)
    lower_factor = jnp.linalg.cholesky(inner_block)
    solved = jax.scipy.linalg.solve_triangular(
        lower_factor, jnp.swapaxes(image_block, 1, 2), lower=True
    )
    return jnp.swapaxes(solved, 1, 2)


def on_device(hidden, norm_gain, proj_weight, start_block):
    layer_count, token_count, width_here = hidden.shape
    mp_count = lax.axis_size("mp")
    count_of_streams = proj_weight.shape[2] // HD
    own_streams = count_of_streams // mp_count
    squares = jnp.sum(jnp.square(hidden.astype(jnp.float32)), axis=2)
    totals = lax.psum(squares, "mp")
    factor = lax.rsqrt(totals / D + epsilon)
    normed = (
        hidden.astype(jnp.float32) * factor[:, :, None] * norm_gain.astype(jnp.float32)[:, None, :]
    ).astype(jnp.bfloat16)
    weight_matrices = proj_weight.reshape(layer_count, width_here, count_of_streams, HD)
    reduced = lax.psum_scatter(
        jnp.einsum(
            "ltw,lwsh->slth", normed, weight_matrices, preferred_element_type=jnp.float32
        ).astype(jnp.bfloat16),
        "mp",
        scatter_dimension=0,
        tiled=True,
    )
    stacked = reduced.transpose(0, 2, 1, 3).reshape(own_streams, token_count, layer_count * HD)
    block_of_basis = lax.dynamic_slice_in_dim(
        start_block, lax.axis_index("mp") * own_streams, own_streams, 0
    ).astype(jnp.float32)
    partial_gram = jnp.einsum("sta,stb->sab", stacked, stacked, preferred_element_type=jnp.float32)
    total_gram_matrix = lax.psum(partial_gram.astype(jnp.bfloat16), "seq").astype(jnp.float32)
    for repeat in range(ITERS):
        block_of_basis = orthonormal_basis(
            jnp.einsum(
                "zcv,zvt->zct", total_gram_matrix, block_of_basis, precision=highest_precision
            )
        )
    basis_half = block_of_basis.astype(jnp.bfloat16)
    return jnp.einsum(
        "sta,sar->tsr", stacked, basis_half, preferred_element_type=jnp.float32
    ).astype(jnp.bfloat16)


def solution(mesh):
    return jax.shard_map(
        on_device,
        mesh=mesh,
        in_specs=(P(None, "seq", "mp"), P(None, "mp"), P(None, "mp", None), P()),
        out_specs=P("seq", "mp", None),
        check_vma=False,
    )
```

profile of v0, /device:TPU:16, one launch (start us, length us, event | category | flops | bytes accessed | tf_op | source)
XLA Modules:
  0.0 324.4 jit_solution(16990641014561848787)
XLA Ops:
  6.5 0.8 convert_element_type.40
  7.3 3.1 fusion
  10.4 14.9 %psum.14 = f32[4,512]{1,0:T(4,128)S(1)} all-reduce(f32[4,512]{1,0:T(4,128)S(1)} %fusion), channel_id=1, replica_groups=mesh['seq'=32,'mp'=8] {'mp'}, use_global_device_ids=true, to_apply=%region_1.0 | all-reduce | flops 2048 | bytes 16384 | tf_op jit(solution)/shard_map/psum | solution.py:30
  25.3 0.0 copy-start.1
  25.3 11.2 %convert_bitcast_fusion = bf16[8,4,512,128]{3,2,0,1:T(8,128)(2,1)} fusion(bf16[4,512,1024]{2,1,0:T(8,128)(2,1)} %param.7, f32[4,1024]{1,0:T(4,128)S(1)} %convert_element_type.40, f32[4,512]{1,0:T(4,128)S(1)} %add_rsqrt_fusion, bf16[4,1024,1024]{2,1,0:T(8,128)(2,1)} %param.9), kind=kOutput, calls=%fused_computation.9 | convolution fusion | flops 4305453056 | bytes 16801792 | tf_op jit(solution)/shard_map/ltw,lwsh->slth/dot_general | solution.py:37
  36.5 0.0 all-reduce.6.cloned.1.call-update
  36.5 0.2 all-reduce.4.cloned.1.call-start
  36.8 0.6 dynamic-slice
  37.4 77.1 %all-reduce.6.cloned.1.call-done = bf16[8,4,512,128]{3,2,0,1:T(8,128)(2,1)} async-done(((bf16[8,4,512,128]{3,2,0,1:T(8,128)(2,1)}), bf16[8,4,512,128]{3,2,0,1:T(8,128)(2,1)}) %all-reduce.6.cloned.1.call-update) | async-done | bytes 4194320
  114.5 1.7 constant_dynamic-slice_fusion
  116.2 0.2 copy.19
  116.4 1.3 convolution_convert_fusion
  117.7 0.0 all-reduce.4.cloned.1.call-update
  117.7 147.6 %all-reduce.4.cloned.1.call-done = bf16[512,512]{1,0:T(8,128)(2,1)} async-done(((bf16[512,512]{1,0:T(8,128)(2,1)}), bf16[512,512]{1,0:T(8,128)(2,1)}) %all-reduce.4.cloned.1.call-update) | async-done | bytes 524304 | tf_op jit(solution)/shard_map/psum | solution.py:49
  265.4 1.3 fusion.20
  266.7 0.6 fusion.30
  267.3 0.1 copy.21
  267.4 11.7 %custom-call.8 = f32[1,128,128]{2,1,0:T(8,128)S(1)} custom-call(f32[1,128,128]{2,1,0:T(8,128)S(1)} %fusion.24), custom_call_target="Cholesky" | custom-call | tf_op jit(solution)/shard_map/jit(cholesky)/cholesky | solution.py:17
  279.2 0.6 compare_reduce_fusion.1
  279.8 0.7 select_select_fusion.1
  280.5 9.8 %custom-call.9 = f32[1,128,128]{1,2,0:T(8,128)S(1)} custom-call(f32[1,128,128]{2,1,0:T(8,128)S(1)} %select_select_fusion.1), custom_call_target="InvertDiagBlocksLowerTriangular" | custom-call | tf_op jit(solution)/shard_map/jit(_solve_triangular)/triangular_solve | solution.py:18
  290.3 0.4 fusion.18
  290.7 1.6 fusion.31
  292.3 0.6 fusion.32
  292.9 0.1 copy.23
  293.1 11.9 %custom-call.10 = f32[1,128,128]{2,1,0:T(8,128)S(1)} custom-call(f32[1,128,128]{2,1,0:T(8,128)S(1)} %fusion.23), custom_call_target="Cholesky" | custom-call | tf_op jit(solution)/shard_map/jit(cholesky)/cholesky | solution.py:17
  305.0 0.6 compare_reduce_fusion
  305.6 0.7 select_select_fusion
  306.3 9.8 %custom-call.11 = f32[1,128,128]{1,2,0:T(8,128)S(1)} custom-call(f32[1,128,128]{2,1,0:T(8,128)S(1)} %select_select_fusion), custom_call_target="InvertDiagBlocksLowerTriangular" | custom-call | tf_op jit(solution)/shard_map/jit(_solve_triangular)/triangular_solve | solution.py:18
  316.1 0.4 fusion.16
  316.5 0.2 fusion.15
  316.8 0.8 copy.24
  (9 shorter events, 0.1 us)
Async XLA Ops:
  6.5 258.8 %copy-start = (bf16[8,512,128]{2,1,0:T(8,128)(2,1)S(1)}, bf16[8,512,128]{2,1,0:T(8,128)(2,1)}, u32[]{:S(2)}) copy-start(bf16[8,512,128]{2,1,0:T(8,128)(2,1)} %param.10) | copy-start | bytes 3145732
  6.5 107.9 %all-reduce.6.cloned.1.call-start = ((), (), s32[]{:S(2)}) async-start(), calls=%async_computation.1 | async-start | bytes 8388608
  25.3 11.5 %copy-start.1 = (u32[256]{0:T(256)S(1)}, u32[256]{0:T(256)}, u32[]{:S(2)}) copy-start(u32[256]{0:T(256)} %constant.50) | copy-start | bytes 3076
  36.5 228.8 %all-reduce.4.cloned.1.call-start = ((), (), s32[]{:S(2)}) async-start(), calls=%async_computation | async-start | bytes 1048576 | tf_op jit(solution)/shard_map/psum | solution.py:49
Sparse Core Ops, SparseCore 0:
  36.6 77.7 all-reduce.5
  117.9 147.4 all-reduce.3
where the time goes:
time: 326 us; the launch traced here: 324 us
  waiting for transfers between devices  225 us (69%)
  other arithmetic  49.8 us (15%)
  matrix products  17.7 us (5%)
  blocking collectives  14.9 us (5%)
  between operations  13.6 us (4%)
  local copies, waits for them, and re-layouts  3.47 us (1%)
    psum x1, waiting for transfers between devices, on_device(): lax.psum(partial_gram.astype(jnp.bfloat16), 'seq').astype(jnp.float32)  148 us
    unnamed x3, waiting for transfers between devices  77.1 us
    another operation x6, other arithmetic, orthonormal_basis(): lower_factor = jnp.linalg.cholesky(inner_block)  25 us
    another operation x4, other arithmetic, orthonormal_basis(): jax.scipy.linalg.solve_triangular(lower_factor, jnp.swapaxes(image_block,...  20.9 us
    psum x1, blocking collectives, on_device(): totals = lax.psum(squares, 'mp')  14.9 us
    dot_general x1, matrix products, on_device(): jnp.einsum('ltw,lwsh->slth', normed, weight_matrices, preferred_element_t...  11.2 us
  transfers between devices with their start and end apart: 2, of which 2 were waited for; matrix products, arithmetic and copies ran while one was open for 0% of the time, Pallas kernels for 0%

commit v1 on v0

v1 whole, which is shorter than its diff:
```python
import jax
import jax.numpy as jnp
from jax import lax
from jax.experimental import pallas as pl
from jax.experimental.pallas import tpu as pltpu
from jax.sharding import PartitionSpec as P

D = 8192
HD = 128
ITERS = 2
LAYERS = 4
NX, NY, NZ = 4, 4, 8
TOK = 512
HALF = TOK // 2
WIDTH = 1024
COLS = LAYERS * HD
LAG = 2
DEPTH = 4

epsilon = 1e-05
highest_precision = lax.Precision.HIGHEST
F32 = jnp.float32
BF16 = jnp.bfloat16


def wide(value):
    return value.astype(F32)


def exchange_kernel(
    hid, gain, weight, out_stacked, out_gram,
    gain_wide, hbuf, wbuf, parts, rcv, x2, xp, xm, rx2, fin,
    lane_sums, sq, sq_rcv, sq_pair, sq_x, row_factor,
    gram_wide, gram_send, ry, zsend, zwide, rz, gfin,
    h_sem, w_sem, pair_s, pair_r, x2_s, x2_r, fin_s, fin_r,
    sqp_s, sqp_r, sqx_s, sqx_r, y_s, y_r, z_s, z_r, gz_s, gz_r, gy_s, gy_r,
):
    seq = lax.axis_index("seq")
    mp = lax.axis_index("mp")
    y, z = seq // NZ, seq % NZ
    x, core = mp // 2, mp % 2

    def at_x(dx):
        return (seq, ((x + dx) % NX) * 2 + core)

    partner = (seq, x * 2 + (1 - core))

    def at_y(dy):
        return (((y + dy) % NY) * NZ + z, mp)

    def at_z(dz):
        return (y * NZ + (z + dz) % NZ, mp)

    def remote(src, dst, s_sem, r_sem, device):
        return pltpu.make_async_remote_copy(
            src_ref=src, dst_ref=dst, send_sem=s_sem, recv_sem=r_sem,
            device_id=device, device_id_type=pl.DeviceIdType.MESH,
        )

    def load_h(l):
        return pltpu.make_async_copy(hid.at[l], hbuf.at[l], h_sem.at[l])

    def load_w(i):
        k, l = i // LAYERS, i % LAYERS
        shift = jnp.where(k == 0, 2, jnp.where(k == 1, 1, jnp.where(k == 2, 3, 0)))
        target = (x + shift) % NX
        start = pl.multiple_of(target * (2 * HD), 2 * HD)
        return pltpu.make_async_copy(weight.at[l, :, pl.ds(start, 2 * HD)], wbuf.at[i], w_sem.at[i])

    for l in range(LAYERS):
        load_h(l).start()
        load_w(l).start()
    barrier = pltpu.get_barrier_semaphore()
    peers = [partner] + [at_x(d) for d in range(1, NX)] + [at_y(d) for d in range(1, NY)] + [at_z(d) for d in range(1, NZ)]
    for peer in peers:
        pl.semaphore_signal(barrier, inc=1, device_id=peer, device_id_type=pl.DeviceIdType.MESH)

    all_gains = wide(gain[...])
    for l in range(LAYERS):
        gain_wide[l] = jnp.broadcast_to(all_gains[l:l + 1, :], (8, WIDTH))

    def pair_copy(i):
        return remote(parts.at[i, 1 - core], rcv.at[i], pair_s.at[i], pair_r.at[i], partner)

    def x2_copy(side, l):
        rows = pl.ds(side * HALF, HALF)
        return remote(x2.at[l, rows], rx2.at[side, l], x2_s.at[side, l], x2_r.at[side, l], at_x(1 if side == 0 else NX - 1))

    def fin_copy(side, half, l):
        rows = pl.ds(half * HALF, HALF)
        source = xp if side == 0 else xm
        return remote(
            source.at[l, rows], fin.at[side, l, rows], fin_s.at[side, half, l], fin_r.at[side, half, l],
            at_x(1 if side == 0 else NX - 1),
        )

    def pair_sum(i, rows):
        return wide(parts[i, core, rows]) + wide(rcv[i, rows])

    ONE = pl.ds(0, HALF)
    TWO = pl.ds(HALF, HALF)

    def scale_rows(l):
        gains = gain_wide[l, 0:1, :]

        def block(b, carry):
            rows = pl.ds(pl.multiple_of(b * 64, 64), 64)
            h = wide(hbuf[l, rows, :])
            square = h * h
            total = square[:, 0:128]
            for c in range(1, WIDTH // 128):
                total = total + square[:, c * 128:(c + 1) * 128]
            lane_sums[l, rows, :] = total
            hbuf[l, rows, :] = (h * gains).astype(BF16)
            return carry

        lax.fori_loop(0, TOK // 64, block, 0)

    def chunk(i, carry):
        l = i % LAYERS

        @pl.when(i < LAYERS)
        def _():
            load_h(l).wait()
            scale_rows(l)

        load_w(i).wait()

        @pl.when(i + DEPTH < 4 * LAYERS)
        def _():
            load_w(i + DEPTH).start()

        for half in range(2):
            rows = pl.ds(half * HALF, HALF)
            product = jnp.dot(hbuf[l, rows, :], wbuf[i], preferred_element_type=F32)
            parts[i, 0, rows] = product[:, :HD].astype(BF16)
            parts[i, 1, rows] = product[:, HD:].astype(BF16)

        @pl.when(i == 0)
        def _():
            pl.semaphore_wait(barrier, len(peers))

        pair_copy(i).start()

        j = i - LAG
        m = j % LAYERS

        @pl.when((j >= 0) & (j < 3 * LAYERS))
        def _():
            pair_copy(j).wait_recv()

        @pl.when((j >= 0) & (j < LAYERS))
        def _():
            x2[m] = pair_sum(j, pl.ds(0, TOK)).astype(BF16)
            x2_copy(0, m).start()
            x2_copy(1, m).start()

        @pl.when((j >= LAYERS) & (j < 2 * LAYERS))
        def _():
            xp[m, TWO] = pair_sum(j, TWO).astype(BF16)
            fin_copy(0, 1, m).start()

        @pl.when((j >= 2 * LAYERS) & (j < 3 * LAYERS))
        def _():
            xm[m, ONE] = pair_sum(j, ONE).astype(BF16)
            fin_copy(1, 0, m).start()

        return carry

    lax.fori_loop(0, 4 * LAYERS, chunk, 0)

    row_id = lax.broadcasted_iota(jnp.int32, (8, HD), 0)

    def one_row(r):
        return jnp.where(row_id == r, 1.0, 0.0).astype(F32)

    squares = jnp.zeros((8, HALF), F32)
    for l in range(LAYERS):
        for half in range(2):
            squares = squares + lax.dot_general(
                one_row(half * LAYERS + l), lane_sums[l, half * HALF:(half + 1) * HALF, :],
                (((1,), (1,)), ((), ())), precision=highest_precision, preferred_element_type=F32,
            )
    sq[...] = squares
    sqp = remote(sq, sq_rcv, sqp_s, sqp_r, partner)
    sqp.start()

    def dependent(l, carry):
        x2_copy(0, l).wait_recv()
        xp[l, ONE] = (pair_sum(LAYERS + l, ONE) + wide(rx2[0, l])).astype(BF16)
        fin_copy(0, 0, l).start()
        x2_copy(1, l).wait_recv()
        xm[l, TWO] = (pair_sum(2 * LAYERS + l, TWO) + wide(rx2[1, l])).astype(BF16)
        fin_copy(1, 1, l).start()
        return carry

    sqp.wait_recv()
    sq_pair[...] = sq[...] + sq_rcv[...]
    sqx = [remote(sq_pair, sq_x.at[d - 1], sqx_s.at[d - 1], sqx_r.at[d - 1], at_x(d)) for d in range(1, NX)]
    for copy in sqx:
        copy.start()

    lax.fori_loop(0, LAYERS, dependent, 0)

    for copy in sqx:
        copy.wait_recv()
    total = sq_pair[...] + sq_x[0] + sq_x[1] + sq_x[2]
    factor = lax.rsqrt(total / D + epsilon)
    for l in range(LAYERS):
        for half in range(2):
            row_factor[l, half * HALF:(half + 1) * HALF, :] = lax.dot_general(
                factor, one_row(half * LAYERS + l),
                (((0,), (0,)), ((), ())), precision=highest_precision, preferred_element_type=F32,
            )

    for l in range(LAYERS):
        pair_copy(3 * LAYERS + l).wait_recv()
        for side in range(2):
            for half in range(2):
                fin_copy(side, half, l).wait_recv()
        everything = pl.ds(0, TOK)
        total = pair_sum(3 * LAYERS + l, everything) + wide(fin[0, l]) + wide(fin[1, l])
        out_stacked[:, l * HD:(l + 1) * HD] = (total * row_factor[l]).astype(BF16)

    for b in range(LAYERS):
        panel = lax.dot_general(
            out_stacked[...], out_stacked[:, b * HD:(b + 1) * HD], (((0,), (0,)), ((), ())), preferred_element_type=F32
        )
        gram_wide[b] = panel
        gram_send[b] = panel.astype(BF16)

    ys = [remote(gram_send.at[(y + d) % NY], ry.at[d - 1], y_s.at[d - 1], y_r.at[d - 1], at_y(d)) for d in range(1, NY)]
    for copy in ys:
        copy.start()
    for copy in ys:
        copy.wait_recv()
    summed = gram_wide[y] + wide(ry[0]) + wide(ry[1]) + wide(ry[2])
    zwide[...] = summed
    zsend[...] = summed.astype(BF16)
    ZR = COLS // NZ

    def z_rows(which):
        return pl.ds(pl.multiple_of(which * ZR, ZR), ZR)

    zs = [
        remote(zsend.at[z_rows((z + d) % NZ)], rz.at[d - 1], z_s.at[d - 1], z_r.at[d - 1], at_z(d))
        for d in range(1, NZ)
    ]
    for copy in zs:
        copy.start()
    for copy in zs:
        copy.wait_recv()
    summed = zwide[z_rows(z)]
    for d in range(1, NZ):
        summed = summed + wide(rz[d - 1])
    gfin[y, z_rows(z)] = summed.astype(BF16)

    gz_out = [
        remote(gfin.at[y, z_rows(z)], gfin.at[y, z_rows(z)], gz_s.at[d - 1], gz_r.at[d - 1], at_z(d))
        for d in range(1, NZ)
    ]
    gz_in = [
        remote(gfin.at[y, z_rows(z)], gfin.at[y, z_rows((z + NZ - d) % NZ)], gz_s.at[d - 1], gz_r.at[d - 1], at_z(d))
        for d in range(1, NZ)
    ]
    for copy in gz_out:
        copy.start()
    for copy in gz_in:
        copy.wait_recv()
    gy_out = [remote(gfin.at[y], gfin.at[y], gy_s.at[d - 1], gy_r.at[d - 1], at_y(d)) for d in range(1, NY)]
    gy_in = [remote(gfin.at[y], gfin.at[(y + NY - d) % NY], gy_s.at[d - 1], gy_r.at[d - 1], at_y(d)) for d in range(1, NY)]
    for copy in gy_out:
        copy.start()
    for copy in gy_in:
        copy.wait_recv()
    for b in range(LAYERS):
        out_gram[:, b * HD:(b + 1) * HD] = gfin[b]

    def drain(i, carry):
        pair_copy(i).wait_send()
        return carry

    lax.fori_loop(0, 4 * LAYERS, drain, 0)

    def drain_x(l, carry):
        for side in range(2):
            x2_copy(side, l).wait_send()
            for half in range(2):
                fin_copy(side, half, l).wait_send()
        return carry

    lax.fori_loop(0, LAYERS, drain_x, 0)
    for copy in [sqp] + sqx + ys + zs + gz_out + gy_out:
        copy.wait_send()


def exchange(hidden, norm_gain, proj_weight):
    dma = pltpu.SemaphoreType.DMA
    vmem = pltpu.VMEM
    return pl.pallas_call(
        exchange_kernel,
        out_shape=(jax.ShapeDtypeStruct((TOK, COLS), BF16), jax.ShapeDtypeStruct((COLS, COLS), BF16)),
        in_specs=[
            pl.BlockSpec(memory_space=pl.ANY),
            pl.BlockSpec(memory_space=pltpu.VMEM),
            pl.BlockSpec(memory_space=pl.ANY),
        ],
        out_specs=(pl.BlockSpec(memory_space=pltpu.VMEM), pl.BlockSpec(memory_space=pltpu.VMEM)),
        scratch_shapes=[
            vmem((LAYERS, 8, WIDTH), F32),
            vmem((LAYERS, TOK, WIDTH), BF16),
            vmem((16, WIDTH, 2 * HD), BF16),
            vmem((16, 2, TOK, HD), BF16),
            vmem((16, TOK, HD), BF16),
            vmem((LAYERS, TOK, HD), BF16),
            vmem((LAYERS, TOK, HD), BF16),
            vmem((LAYERS, TOK, HD), BF16),
            vmem((2, LAYERS, HALF, HD), BF16),
            vmem((2, LAYERS, TOK, HD), BF16),
            vmem((LAYERS, TOK, HD), F32),
            vmem((8, HALF), F32),
            vmem((8, HALF), F32),
            vmem((8, HALF), F32),
            vmem((NX - 1, 8, HALF), F32),
            vmem((LAYERS, TOK, HD), F32),
            vmem((LAYERS, COLS, HD), F32),
            vmem((LAYERS, COLS, HD), BF16),
            vmem((NY - 1, COLS, HD), BF16),
            vmem((COLS, HD), BF16),
            vmem((COLS, HD), F32),
            vmem((NZ - 1, COLS // NZ, HD), BF16),
            vmem((NY, COLS, HD), BF16),
            dma((LAYERS,)), dma((16,)), dma((16,)), dma((16,)),
            dma((2, LAYERS)), dma((2, LAYERS)), dma((2, 2, LAYERS)), dma((2, 2, LAYERS)),
            dma, dma, dma((NX - 1,)), dma((NX - 1,)),
            dma((NY - 1,)), dma((NY - 1,)), dma((NZ - 1,)), dma((NZ - 1,)),
            dma((NZ - 1,)), dma((NZ - 1,)), dma((NY - 1,)), dma((NY - 1,)),
        ],
        compiler_params=pltpu.CompilerParams(
            collective_id=0, has_side_effects=True, vmem_limit_bytes=56 * 1024 * 1024
        ),
    )(hidden, norm_gain, proj_weight)


def orthonormal_basis(image_block):
    inner_block = jnp.einsum("sar,saq->srq", image_block, image_block, precision=highest_precision)
    lower_factor = jnp.linalg.cholesky(inner_block)
    solved = jax.scipy.linalg.solve_triangular(
        lower_factor, jnp.swapaxes(image_block, 1, 2), lower=True
    )
    return jnp.swapaxes(solved, 1, 2)


def on_device(hidden, norm_gain, proj_weight, start_block):
    stacked, gram = exchange(hidden, norm_gain, proj_weight)
    block_of_basis = lax.dynamic_slice_in_dim(start_block, lax.axis_index("mp"), 1, 0).astype(F32)
    total_gram_matrix = gram.astype(F32)[None]
    for repeat in range(ITERS):
        block_of_basis = orthonormal_basis(
            jnp.einsum("zcv,zvt->zct", total_gram_matrix, block_of_basis, precision=highest_precision)
        )
    basis_half = block_of_basis.astype(BF16)
    return jnp.einsum("sta,sar->tsr", stacked[None], basis_half, preferred_element_type=F32).astype(BF16)


def solution(mesh):
    return jax.shard_map(
        on_device,
        mesh=mesh,
        in_specs=(P(None, "seq", "mp"), P(None, "mp"), P(None, "mp", None), P()),
        out_specs=P("seq", "mp", None),
        check_vma=False,
    )
```

time: 326 us -> 112 us (0.34)
  waiting for transfers between devices: 225 us -> 0 us
  Pallas kernels: 0 us -> 58.5 us
  blocking collectives: 14.9 us -> 0 us
  between operations: 13.6 us -> 0.12 us
  matrix products: 17.7 us -> 6.34 us
  other arithmetic: 49.8 us -> 45.9 us
    psum x1 -> x0, waiting for transfers between devices: 148 us -> none  [on_device(): lax.psum(partial_gram.astype(jnp.bfloat16), 'seq').astype(jnp.float32)]
    unnamed x3 -> x0, waiting for transfers between devices: 77.1 us -> none
    pallas_call x0 -> x1, Pallas kernels: none -> 58.5 us  [exchange(): pl.pallas_call(exchange_kernel, out_shape=(jax.ShapeDtypeStruct((TOK, COL...]
    psum x1 -> x0, blocking collectives: 14.9 us -> none  [on_device(): totals = lax.psum(squares, 'mp')]
    dot_general x3 -> x1, matrix products: 12.7 us -> 1.35 us  [on_device(): jnp.einsum('sta,sar->tsr', stacked[None], basis_half, preferred_element_t...]
  transfers between devices with their start and end apart: 2 -> 0, of which waited for: 2 -> 0; matrix products, arithmetic and copies ran while one was open for 0% -> 0% of each run, Pallas kernels for 0% -> 0%
where the time goes in v1:
time: 112 us
  Pallas kernels  58.5 us (52%)
  other arithmetic  45.9 us (41%)
  matrix products  6.34 us (6%)
    pallas_call x1, Pallas kernels, exchange(): pl.pallas_call(exchange_kernel, out_shape=(jax.ShapeDtypeStruct((TOK, COL...  58.5 us
    another operation x6, other arithmetic, orthonormal_basis(): lower_factor = jnp.linalg.cholesky(inner_block)  25 us
    another operation x4, other arithmetic, orthonormal_basis(): jax.scipy.linalg.solve_triangular(lower_factor, jnp.swapaxes(image_block,...  20.9 us
    dot_general x2, matrix products, on_device(): jnp.einsum('zcv,zvt->zct', total_gram_matrix, block_of_basis, precision=h...  2.99 us

profile of v1, /device:TPU:16, one launch (start us, length us, event | category | flops | bytes accessed | tf_op | source)
XLA Modules:
  0.0 111.8 jit_solution(2368981625704194622)
XLA Ops:
  0.0 0.0 copy-start
  0.0 58.5 %shard_map.46 = (bf16[512,512]{1,0:T(8,128)(2,1)}, bf16[512,512]{1,0:T(8,128)(2,1)}) custom-call(bf16[4,512,1024]{2,1,0:T(8,128)(2,1)} %hid.1, bf16[4,1024]{1,0:T(4,128)(2,1)} %gain.1, bf16[4,1024,1024]{2,1,0:T(8,128)(2,1)} %weight.1), custom_call_target="tpu_custom_call" | custom-call | tf_op jit(solution)/shard_map/pallas_call | solution.py:300
  58.5 0.0 copy-done
  58.5 1.3 %fusion.6 = f32[512,128]{1,0:T(8,128)S(1)} fusion(bf16[512,512]{1,0:T(8,128)(2,1)} %get-tuple-element.9, bf16[8,512,128]{2,1,0:T(8,128)(2,1)S(1)} %copy-done, s32[]{:T(128)S(6)} %select_n.6), kind=kOutput, calls=%fused_computation.8 | convolution fusion | flops 67108864 | bytes 917508 | tf_op jit(solution)/shard_map/zcv,zvt->zct/dot_general | solution.py:360
  59.8 0.6 fusion.16
  60.4 0.1 copy.6
  60.5 11.7 %custom-call.8 = f32[1,128,128]{2,1,0:T(8,128)S(1)} custom-call(f32[1,128,128]{2,1,0:T(8,128)S(1)} %fusion.10), custom_call_target="Cholesky" | custom-call | tf_op jit(solution)/shard_map/jit(cholesky)/cholesky | solution.py:347
  72.3 0.6 compare_reduce_fusion.1
  72.9 0.7 select_select_fusion.1
  73.6 9.8 %custom-call.9 = f32[1,128,128]{1,2,0:T(8,128)S(1)} custom-call(f32[1,128,128]{2,1,0:T(8,128)S(1)} %select_select_fusion.1), custom_call_target="InvertDiagBlocksLowerTriangular" | custom-call | tf_op jit(solution)/shard_map/jit(_solve_triangular)/triangular_solve | solution.py:348
  83.4 0.4 fusion.4
  83.8 1.6 %fusion.17 = f32[512,128]{1,0:T(8,128)S(1)} fusion(bf16[512,512]{1,0:T(8,128)(2,1)} %get-tuple-element.9, f32[128,512]{1,0:T(8,128)S(1)} %fusion.4), kind=kOutput, calls=%fused_computation.28 | convolution fusion | flops 402653184 | bytes 1048576 | tf_op jit(solution)/shard_map/zcv,zvt->zct/dot_general | solution.py:360
  85.5 0.6 fusion.18
  86.1 0.1 copy.8
  86.2 11.9 %custom-call.10 = f32[1,128,128]{2,1,0:T(8,128)S(1)} custom-call(f32[1,128,128]{2,1,0:T(8,128)S(1)} %fusion.9), custom_call_target="Cholesky" | custom-call | tf_op jit(solution)/shard_map/jit(cholesky)/cholesky | solution.py:347
  98.1 0.6 compare_reduce_fusion
  98.8 0.7 select_select_fusion
  99.4 9.8 %custom-call.11 = f32[1,128,128]{1,2,0:T(8,128)S(1)} custom-call(f32[1,128,128]{2,1,0:T(8,128)S(1)} %select_select_fusion), custom_call_target="InvertDiagBlocksLowerTriangular" | custom-call | tf_op jit(solution)/shard_map/jit(_solve_triangular)/triangular_solve | solution.py:348
  109.2 0.4 fusion.2
  109.7 1.3 %fusion.1 = bf16[512,1,128]{0,2,1:T(8,128)(2,1)S(1)} fusion(bf16[512,128]{0,1:T(8,128)(2,1)S(1)} %fusion.2, bf16[512,512]{1,0:T(8,128)(2,1)} %get-tuple-element.10), kind=kOutput, calls=%fused_computation.3 | convolution fusion | flops 67174400 | bytes 786432 | tf_op jit(solution)/shard_map/sta,sar->tsr/dot_general | solution.py:363
  111.0 0.8 copy.9
  (4 shorter events, 0.1 us)
Async XLA Ops:
  0.0 58.5 %copy-start = (bf16[8,512,128]{2,1,0:T(8,128)(2,1)S(1)}, bf16[8,512,128]{2,1,0:T(8,128)(2,1)}, u32[]{:S(2)}) copy-start(bf16[8,512,128]{2,1,0:T(8,128)(2,1)} %param.10) | copy-start | bytes 3145732

commit v2 on v1

--- a/solution.py
+++ b/solution.py
@@ -27,12 +27,66 @@
     return value.astype(F32)
 
 
+def product(a, b, contract_a, contract_b, precision=None):
+    return lax.dot_general(
+        a, b, (((contract_a,), (contract_b,)), ((), ())), precision=precision, preferred_element_type=F32
+    )
+
+
+def inverse_cholesky(inner):
+    n = inner.shape[0]
+    lane = lax.broadcasted_iota(jnp.int32, (8, n), 1)
+    sub = lax.broadcasted_iota(jnp.int32, (8, n), 0)
+    blocks = [inner[8 * i:8 * i + 8] for i in range(n // 8)]
+    for v in range(n // 8):
+        first = 8 * v
+        pivot_columns = (lane >= first) & (lane < first + 8)
+        column = [jnp.broadcast_to(blocks[v][:, first + t:first + t + 1], (8, n)) for t in range(8)]
+        s = [[column[t][i:i + 1, :] for t in range(i + 1)] for i in range(8)]
+        row = [
+            jnp.where(pivot_columns[0:1], jnp.where(lane[0:1] == first + t, 1.0, 0.0), blocks[v][t:t + 1, :])
+            for t in range(8)
+        ]
+        inverse = [None] * 8
+        m = [[None] * 8 for _ in range(8)]
+        for t in range(8):
+            inverse[t] = 1.0 / s[t][t]
+            for i in range(t + 1, 8):
+                m[i][t] = s[i][t] * inverse[t]
+            for i in range(t + 1, 8):
+                for u in range(t + 1, i + 1):
+                    s[i][u] = s[i][u] - m[i][t] * s[u][t]
+            for i in range(t + 1, 8):
+                row[i] = row[i] - m[i][t] * row[t]
+        scaled = [row[t] * inverse[t] for t in range(8)]
+        done = blocks[v]
+        for t in range(8):
+            done = jnp.where(sub == t, jnp.where(lane[0:1] == first + t, s[t][t], row[t]), done)
+        blocks[v] = done
+        for k in range(v + 1, n // 8):
+            old = [jnp.broadcast_to(blocks[k][:, first + t:first + t + 1], (8, n)) for t in range(8)]
+            new = jnp.where(pivot_columns, 0.0, blocks[k])
+            for t in range(8):
+                for u in range(t):
+                    old[t] = old[t] - m[t][u] * old[u]
+                new = new - old[t] * scaled[t]
+            blocks[k] = new
+    rows = []
+    for k in range(n // 8):
+        diagonal = lane == sub + 8 * k
+        pivots = jnp.sum(jnp.where(diagonal, blocks[k], 0.0), axis=1, keepdims=True)
+        unit = jnp.where(lane < sub + 8 * k, blocks[k], jnp.where(diagonal, 1.0, 0.0))
+        rows.append(unit * lax.rsqrt(pivots))
+    return jnp.concatenate(rows, axis=0)
+
+
 def exchange_kernel(
-    hid, gain, weight, out_stacked, out_gram,
+    hid, gain, weight, start, out,
+    stacked, gram, start_here, basis, image,
     gain_wide, hbuf, wbuf, parts, rcv, x2, xp, xm, rx2, fin,
     lane_sums, sq, sq_rcv, sq_pair, sq_x, row_factor,
     gram_wide, gram_send, ry, zsend, zwide, rz, gfin,
-    h_sem, w_sem, pair_s, pair_r, x2_s, x2_r, fin_s, fin_r,
+    b_sem, h_sem, w_sem, pair_s, pair_r, x2_s, x2_r, fin_s, fin_r,
     sqp_s, sqp_r, sqx_s, sqx_r, y_s, y_r, z_s, z_r, gz_s, gz_r, gy_s, gy_r,
 ):
     seq = lax.axis_index("seq")
@@ -70,6 +124,8 @@
     for l in range(LAYERS):
         load_h(l).start()
         load_w(l).start()
+    load_start = pltpu.make_async_copy(start.at[mp], start_here, b_sem)
+    load_start.start()
     barrier = pltpu.get_barrier_semaphore()
     peers = [partner] + [at_x(d) for d in range(1, NX)] + [at_y(d) for d in range(1, NY)] + [at_z(d) for d in range(1, NZ)]
     for peer in peers:
@@ -220,11 +276,11 @@
                 fin_copy(side, half, l).wait_recv()
         everything = pl.ds(0, TOK)
         total = pair_sum(3 * LAYERS + l, everything) + wide(fin[0, l]) + wide(fin[1, l])
-        out_stacked[:, l * HD:(l + 1) * HD] = (total * row_factor[l]).astype(BF16)
+        stacked[:, l * HD:(l + 1) * HD] = (total * row_factor[l]).astype(BF16)
 
     for b in range(LAYERS):
         panel = lax.dot_general(
-            out_stacked[...], out_stacked[:, b * HD:(b + 1) * HD], (((0,), (0,)), ((), ())), preferred_element_type=F32
+            stacked[...], stacked[:, b * HD:(b + 1) * HD], (((0,), (0,)), ((), ())), preferred_element_type=F32
         )
         gram_wide[b] = panel
         gram_send[b] = panel.astype(BF16)
@@ -274,7 +330,25 @@
     for copy in gy_in:
         copy.wait_recv()
     for b in range(LAYERS):
-        out_gram[:, b * HD:(b + 1) * HD] = gfin[b]
+        gram[:, b * HD:(b + 1) * HD] = gfin[b]
+
+    load_start.wait()
+    basis[...] = wide(start_here[...])
+
+    def power_step(repeat, carry):
+        held = basis[...]
+        high = held.astype(BF16)
+        rest = held - wide(high)
+        middle = rest.astype(BF16)
+        low = (rest - wide(middle)).astype(BF16)
+        whole = gram[...]
+        image[...] = product(whole, high, 1, 0) + product(whole, middle, 1, 0) + product(whole, low, 1, 0)
+        inner = product(image[...], image[...], 0, 0, highest_precision)
+        basis[...] = product(image[...], inverse_cholesky(inner), 1, 1, highest_precision)
+        return carry
+
+    lax.fori_loop(0, ITERS, power_step, 0)
+    out[...] = product(stacked[...], basis[...].astype(BF16), 1, 0).astype(BF16)
 
     def drain(i, carry):
         pair_copy(i).wait_send()
@@ -294,19 +368,25 @@
         copy.wait_send()
 
 
-def exchange(hidden, norm_gain, proj_weight):
+def on_device(hidden, norm_gain, proj_weight, start_block):
     dma = pltpu.SemaphoreType.DMA
     vmem = pltpu.VMEM
-    return pl.pallas_call(
+    latents = pl.pallas_call(
         exchange_kernel,
-        out_shape=(jax.ShapeDtypeStruct((TOK, COLS), BF16), jax.ShapeDtypeStruct((COLS, COLS), BF16)),
+        out_shape=jax.ShapeDtypeStruct((TOK, HD), BF16),
         in_specs=[
             pl.BlockSpec(memory_space=pl.ANY),
             pl.BlockSpec(memory_space=pltpu.VMEM),
             pl.BlockSpec(memory_space=pl.ANY),
+            pl.BlockSpec(memory_space=pl.ANY),
         ],
-        out_specs=(pl.BlockSpec(memory_space=pltpu.VMEM), pl.BlockSpec(memory_space=pltpu.VMEM)),
+        out_specs=pl.BlockSpec(memory_space=pltpu.VMEM),
         scratch_shapes=[
+            vmem((TOK, COLS), BF16),
+            vmem((COLS, COLS), BF16),
+            vmem((COLS, HD), BF16),
+            vmem((COLS, HD), F32),
+            vmem((COLS, HD), F32),
             vmem((LAYERS, 8, WIDTH), F32),
             vmem((LAYERS, TOK, WIDTH), BF16),
             vmem((16, WIDTH, 2 * HD), BF16),
@@ -330,7 +410,7 @@
             vmem((COLS, HD), F32),
             vmem((NZ - 1, COLS // NZ, HD), BF16),
             vmem((NY, COLS, HD), BF16),
-            dma((LAYERS,)), dma((16,)), dma((16,)), dma((16,)),
+            dma, dma((LAYERS,)), dma((16,)), dma((16,)), dma((16,)),
             dma((2, LAYERS)), dma((2, LAYERS)), dma((2, 2, LAYERS)), dma((2, 2, LAYERS)),
             dma, dma, dma((NX - 1,)), dma((NX - 1,)),
             dma((NY - 1,)), dma((NY - 1,)), dma((NZ - 1,)), dma((NZ - 1,)),
@@ -339,28 +419,8 @@
         compiler_params=pltpu.CompilerParams(
             collective_id=0, has_side_effects=True, vmem_limit_bytes=56 * 1024 * 1024
         ),
-    )(hidden, norm_gain, proj_weight)
-
-
-def orthonormal_basis(image_block):
-    inner_block = jnp.einsum("sar,saq->srq", image_block, image_block, precision=highest_precision)
-    lower_factor = jnp.linalg.cholesky(inner_block)
-    solved = jax.scipy.linalg.solve_triangular(
-        lower_factor, jnp.swapaxes(image_block, 1, 2), lower=True
-    )
-    return jnp.swapaxes(solved, 1, 2)
-
-
-def on_device(hidden, norm_gain, proj_weight, start_block):
-    stacked, gram = exchange(hidden, norm_gain, proj_weight)
-    block_of_basis = lax.dynamic_slice_in_dim(start_block, lax.axis_index("mp"), 1, 0).astype(F32)
-    total_gram_matrix = gram.astype(F32)[None]
-    for repeat in range(ITERS):
-        block_of_basis = orthonormal_basis(
-            jnp.einsum("zcv,zvt->zct", total_gram_matrix, block_of_basis, precision=highest_precision)
-        )
-    basis_half = block_of_basis.astype(BF16)
-    return jnp.einsum("sta,sar->tsr", stacked[None], basis_half, preferred_element_type=F32).astype(BF16)
+    )(hidden, norm_gain, proj_weight, start_block)
+    return latents.reshape(TOK, 1, HD)
 
 
 def solution(mesh):

time: 112 us -> 70.1 us (0.63)
  other arithmetic: 45.9 us -> 0 us
  Pallas kernels: 58.5 us -> 68.4 us
  matrix products: 6.34 us -> 0 us
    another operation x10 -> x0, other arithmetic: 45.9 us -> none  [the longest x6 25 us: orthonormal_basis(): lower_factor = jnp.linalg.cholesky(inner_block)]
    pallas_call x1, Pallas kernels: 58.5 us -> 68.4 us  [on_device(): pl.pallas_call(exchange_kernel, out_shape=jax.ShapeDtypeStruct((TOK, HD),...]
    dot_general x5 -> x0, matrix products: 5.51 us -> none  [the longest x2 2.99 us: on_device(): jnp.einsum('zcv,zvt->zct', total_gram_matrix, block_of_basis, precision=h...]
    unnamed x2 -> x1, local copies, waits for them, and re-layouts: 0.01 us -> 1.57 us
where the time goes in v2:
time: 70.1 us; the launch traced here: 69.9 us
  Pallas kernels  68.4 us (98%)
  local copies, waits for them, and re-layouts  1.57 us (2%)
    pallas_call x1, Pallas kernels, on_device(): pl.pallas_call(exchange_kernel, out_shape=jax.ShapeDtypeStruct((TOK, HD),...  68.4 us
    unnamed x1, local copies, waits for them, and re-layouts  1.57 us

profile of v2, /device:TPU:16, one launch (start us, length us, event | category | flops | bytes accessed | tf_op | source)
XLA Modules:
  0.0 69.9 jit_solution(5475412853202399033)
XLA Ops:
  0.0 68.4 %shard_map.46 = bf16[512,128]{1,0:T(8,128)(2,1)} custom-call(bf16[4,512,1024]{2,1,0:T(8,128)(2,1)} %hid.1, bf16[4,1024]{1,0:T(4,128)(2,1)} %gain.1, bf16[4,1024,1024]{2,1,0:T(8,128)(2,1)} %weight.1, bf16[8,512,128]{2,1,0:T(8,128)(2,1)} %start.1), custom_call_target="tpu_custom_call" | custom-call | tf_op jit(solution)/shard_map/pallas_call | solution.py:374
  68.4 1.6 %copy.6 = bf16[512,1,128]{2,0,1:T(8,128)(2,1)} copy(bf16[512,1,128]{2,0,1:T(8,128)(2,1)} %bitcast.1) | data formatting | bytes 262144
